TPU v7x, 128 devices: a whole 4x4x4 slice. The times are simulated.
128 devices in a mesh: row: 32 (over x, y, core), col: 4 (over z).
Axes of the slice: x: 4, y: 4, z: 4, core: 2. Of those that a mesh axis runs over, the one named last changes fastest.
Arguments:
- right_side: bfloat16 [65536, 4096], P(('row', 'col')), may hold values from -6 to 6
- factor: bfloat16 [65536, 2048], P(('row', 'col')), may hold values from -0.125 to 0.125
- diag_inverse: bfloat16 [2048, 512], P('col'), as said below
- tile_mask: int32 [128, 4], P(('row', 'col')), may hold values from 0 to 1, as said below
- window_rows: int32 [4], replicated, may hold values from 0 to 127, as said below
Outputs:
- solution: bfloat16 [2048, 4096], P('row', 'col')
- updated_rhs: bfloat16 [65536, 4096], P(('row', 'col'))
Inputs may be any that keep to these rules, and one draw needn't show every extreme that they name: `window_rows`: distinct stored panel numbers, panels 0 and 127 always among them; panel p is stored on device p // 1 of row+col, and the window panels lie on different devices. `tile_mask`: 0 or 1; in the row of window panel k the entries of columns k and beyond are 0. `diag_inverse`: each tile is lower triangular.
All inputs are finite; a program needn't handle non-finite values.
Results may differ from a plain program's by a relative error of at most 0.0056.
Values may be sent and summed in bfloat16 or wider, within the bound.
A program may use at most 128 MiB of HBM per device.

v0:
```python
import jax
import jax.numpy as jnp
from jax import lax
from jax.sharding import PartitionSpec as P

AXES = ("row", "col")
NT = (((1,), (1,)), ((), ()))


def dot_nt(a, b):
    return lax.dot_general(a, b, NT, preferred_element_type=jnp.float32)


def body(right_side, factor, diag_inverse, tile_mask, window_rows):
    panel = diag_inverse.shape[1]
    window = factor.shape[1] // panel
    columns = right_side.shape[1]
    ncol = lax.axis_size("col")
    nrow = lax.axis_size("row")
    ndev = nrow * ncol
    width = columns // ndev
    col_index = lax.axis_index("col")
    row_index = lax.axis_index("row")
    me = row_index * ncol + col_index
    present = jnp.repeat(tile_mask[0] > 0, panel)
    masked = jnp.where(present[None, :], factor, jnp.zeros_like(factor))
    pieces = lax.all_to_all(
        right_side.T.reshape(ndev, width, panel), AXES, split_axis=0, concat_axis=0, tiled=True
    )
    lower = []
    for k in range(1, window):
        mine = me == window_rows[k]
        for j in range(k):
            tile = masked[:, j * panel : (j + 1) * panel]
            lower.append(jnp.where(mine, tile, jnp.zeros_like(tile)))
    lower = lax.psum(jnp.stack(lower), AXES)
    inverses = lax.all_gather(diag_inverse, "col", axis=0, tiled=True).reshape(window, panel, panel)
    solved = []
    for k in range(window):
        residual = lax.dynamic_index_in_dim(pieces, window_rows[k], 0, keepdims=False).astype(
            jnp.float32
        )
        for j in range(k):
            residual = residual - dot_nt(solved[j], lower[k * (k - 1) // 2 + j])
        solved.append(dot_nt(residual.astype(jnp.bfloat16), inverses[k]).astype(jnp.bfloat16))
    whole = lax.all_gather(jnp.concatenate(solved, axis=1), AXES, axis=0, tiled=True)
    updated = (right_side.astype(jnp.float32) - dot_nt(masked, whole)).astype(jnp.bfloat16)
    block_rows = window * panel // nrow
    block_cols = columns // ncol
    solution = lax.dynamic_slice(
        whole, (col_index * block_cols, row_index * block_rows), (block_cols, block_rows)
    ).T
    return (solution, updated)


def solution(mesh):
    in_specs = (P(AXES, None), P(AXES, None), P("col", None), P(AXES, None), P())
    out_specs = (P("row", "col"), P(AXES, None))
    return jax.shard_map(body, mesh=mesh, in_specs=in_specs, out_specs=out_specs, check_vma=False)
```

profile of v0, /device:TPU:1, one launch (start us, length us, event | category | flops | bytes accessed | tf_op | source)
XLA Modules:
  0.0 338.8 jit_solution(7828299529200578639)
XLA Ops:
  8.0 0.0 all-gather.3.cloned.1.call-start
  8.0 0.7 all-gather.3.cloned.1.call-update
  8.7 6.4 %copy.8 = bf16[512,4096]{0,1:T(8,128)(2,1)} copy(bf16[512,4096]{1,0:T(8,128)(2,1)} %param.5) | data formatting | bytes 8388608 | tf_op args[0]
  15.1 0.0 copy-start.1
  15.1 0.0 copy-start
  15.1 12.0 %all-to-all-start = ((bf16[128,32,512]{2,1,0:T(8,128)(2,1)}), bf16[128,32,512]{2,1,0:T(8,128)(2,1)}, u32[]{:S(2)}, u32[]{:S(2)}) async-start(bf16[128,32,512]{2,1,0:T(8,128)(2,1)} %bitcast.72), calls=%async_computation | async-start | bytes 8388608 | tf_op jit(solution)/shard_map/all_to_all | solution.py:27
  27.1 0.0 all-reduce.2.cloned.1.call-start
  27.2 0.0 copy-done.1
  27.2 0.1 broadcast_bitcast_fusion
  27.3 0.0 copy-done
  27.3 0.6 fusion.16
  29.8 1.8 broadcast_select_fusion
  31.5 0.9 bitcast_dynamic-update-slice_fusion.4
  32.5 1.0 bitcast_dynamic-update-slice_fusion.3
  33.4 0.9 bitcast_dynamic-update-slice_fusion.2
  34.3 0.9 bitcast_dynamic-update-slice_fusion.1
  35.3 0.9 bitcast_dynamic-update-slice_fusion
  36.2 0.9 fusion.7
  37.1 0.0 all-reduce.2.cloned.1.call-update
  37.1 0.0 all-gather.5.cloned.1.call-start
  44.7 46.7 %all-gather.3.cloned.1.call-done = bf16[2048,512]{1,0:T(8,128)(2,1)} async-done(((bf16[512,512]{1,0:T(8,128)(2,1)}), bf16[2048,512]{1,0:T(8,128)(2,1)}) %all-gather.3.cloned.1.call-update) | async-done | bytes 2097168 | tf_op jit(solution)/shard_map/all_gather | solution.py:37
  91.4 0.0 all-to-all-done
  91.4 1.3 convolution_convert_fusion.3
  92.7 133.6 %all-reduce.2.cloned.1.call-done = bf16[6,512,512]{2,1,0:T(8,128)(2,1)} async-done(((bf16[6,512,512]{2,1,0:T(8,128)(2,1)}), bf16[6,512,512]{2,1,0:T(8,128)(2,1)}) %all-reduce.2.cloned.1.call-update) | async-done | bytes 3145744 | tf_op jit(solution)/shard_map/psum | solution.py:36
  226.3 1.3 convolution_subtract_fusion.4
  227.6 1.6 convolution_convert_fusion.2
  229.3 1.3 convolution_subtract_fusion.2
  230.6 1.6 convolution_convert_fusion.1
  232.2 1.3 convolution_subtract_fusion.1
  233.6 1.6 convolution_convert_fusion
  235.2 0.7 pad_maximum_fusion
  235.9 0.0 all-gather.5.cloned.1.call-update
  235.9 79.1 %all-gather.5.cloned.1.call-done = bf16[4096,2048]{1,0:T(8,128)(2,1)} async-done(((bf16[32,2048]{1,0:T(8,128)(2,1)}), bf16[4096,2048]{1,0:T(8,128)(2,1)}) %all-gather.5.cloned.1.call-update) | async-done | bytes 16777232 | tf_op jit(solution)/shard_map/all_gather | solution.py:46
  315.1 1.1 dynamic-slice_bitcast_fusion
  316.2 0.8 copy.9
  317.0 14.4 %subtract_convert_fusion = bf16[512,4096]{1,0:T(8,128)(2,1)} fusion(bf16[512,4096]{1,0:T(8,128)(2,1)} %param.5, bf16[512,2048]{1,0:T(8,128)(2,1)S(1)} %broadcast_select_fusion, bf16[4096,2048]{1,0:T(8,128)(2,1)} %all-gather.5.cloned.1.call-done), kind=kOutput, calls=%fused_computation | convolution fusion | flops 8596226048 | bytes 27262976 | tf_op jit(solution)/shard_map/dot_general | solution.py:11
  (2 shorter events, 0.0 us)
Async XLA Ops:
  8.0 83.4 %all-gather.3.cloned.1.call-start = ((), (), s32[]{:S(2)}) async-start(), calls=%async_computation.1 | async-start | bytes 2621440 | tf_op jit(solution)/shard_map/all_gather | solution.py:37
  15.1 12.0 %copy-start.1 = (s32[1,4]{1,0:T(1,128)S(1)}, s32[1,4]{1,0:T(1,128)}, u32[]{:S(2)}) copy-start(s32[1,4]{1,0:T(1,128)} %param.8) | copy-start | bytes 52
  15.1 12.1 %copy-start = (s32[4]{0:T(128)S(1)}, s32[4]{0:T(128)}, u32[]{:S(2)}) copy-start(s32[4]{0:T(128)} %param.9) | copy-start | bytes 52
  15.1 76.2 %all-to-all-start = ((bf16[128,32,512]{2,1,0:T(8,128)(2,1)}), bf16[128,32,512]{2,1,0:T(8,128)(2,1)}, u32[]{:S(2)}, u32[]{:S(2)}) async-start(bf16[128,32,512]{2,1,0:T(8,128)(2,1)} %bitcast.72), calls=%async_computation | async-start | bytes 8388608 | tf_op jit(solution)/shard_map/all_to_all | solution.py:27
  27.1 199.2 %all-reduce.2.cloned.1.call-start = ((), (), s32[]{:S(2)}) async-start(), calls=%async_computation.2 | async-start | bytes 6291456 | tf_op jit(solution)/shard_map/psum | solution.py:36
  37.1 278.0 %all-gather.5.cloned.1.call-start = ((), (), s32[]{:S(2)}) async-start(), calls=%async_computation.3 | async-start | bytes 16908288 | tf_op jit(solution)/shard_map/all_gather | solution.py:46
Sparse Core Ops, SparseCore 0:
  10.6 80.7 all-gather.2
Sparse Core Ops, SparseCore 1:
  37.2 189.1 all-reduce.1
  236.0 79.0 all-gather.4
where the time goes:
time: 339 us
  waiting for transfers between devices  260 us (77%)
  between operations  25 us (7%)
  matrix products  24.5 us (7%)
  starting transfers between devices  12.1 us (4%)
  local copies, waits for them, and re-layouts  9 us (3%)
  other arithmetic  8.01 us (2%)
    psum x1, waiting for transfers between devices, body(): lower = lax.psum(jnp.stack(lower), AXES)  134 us
    all_gather x1, waiting for transfers between devices, body(): lax.all_gather(jnp.concatenate(solved, axis=1), AXES, axis=0, tiled=True)  79.1 us
    all_gather x1, waiting for transfers between devices, body(): lax.all_gather(diag_inverse, 'col', axis=0, tiled=True)  46.7 us
    dot_general x8, matrix products, dot_nt(): return lax.dot_general(a, b, NT, preferred_element_type=jnp.float32)  24.5 us
    all_to_all x1, starting transfers between devices, body(): lax.all_to_all(right_side.T.reshape(ndev, width, panel), AXES, split_axis...  12 us
    unnamed x8, local copies, waits for them, and re-layouts  7.29 us
  transfers between devices with their start and end apart: 4, of which 3 were waited for; matrix products, arithmetic and copies ran while one was open for 5% of the time, Pallas kernels for 0%

commit v1 on v0

--- a/solution.py
+++ b/solution.py
@@ -5,6 +5,22 @@
 
 AXES = ("row", "col")
 NT = (((1,), (1,)), ((), ()))
+
+
+def gather_around(x, axis, dim):
+    ways, here, lap = (lax.axis_size(axis), lax.axis_index(axis), x.shape[dim])
+    shape = [n * ways if d == dim else n for d, n in enumerate(x.shape)]
+    full = lax.dynamic_update_slice_in_dim(jnp.zeros(shape, x.dtype), x, here * lap, axis=dim)
+    going_up = going_down = x
+    for far in range(1, ways // 2 + 1):
+        going_up = lax.ppermute(going_up, axis, [(d, (d + 1) % ways) for d in range(ways)])
+        full = lax.dynamic_update_slice_in_dim(full, going_up, (here - far) % ways * lap, axis=dim)
+        if 2 * far < ways:
+            going_down = lax.ppermute(going_down, axis, [(d, (d - 1) % ways) for d in range(ways)])
+            full = lax.dynamic_update_slice_in_dim(
+                full, going_down, (here + far) % ways * lap, axis=dim
+            )
+    return full
 
 
 def dot_nt(a, b):
@@ -34,7 +50,7 @@
             tile = masked[:, j * panel : (j + 1) * panel]
             lower.append(jnp.where(mine, tile, jnp.zeros_like(tile)))
     lower = lax.psum(jnp.stack(lower), AXES)
-    inverses = lax.all_gather(diag_inverse, "col", axis=0, tiled=True).reshape(window, panel, panel)
+    inverses = gather_around(diag_inverse, "col", 0).reshape(window, panel, panel)
     solved = []
     for k in range(window):
         residual = lax.dynamic_index_in_dim(pieces, window_rows[k], 0, keepdims=False).astype(

time: 339 us -> 329 us (0.971)
  waiting for transfers between devices: 260 us -> 241 us
  local copies, waits for them, and re-layouts: 9 us -> 15.9 us
    ppermute x0 -> x3, waiting for transfers between devices: none -> 51.5 us  [the longest x2 51.5 us: gather_around(): lax.ppermute(going_up, axis, [(d, (d + 1) % ways) for d in range(ways)])]
    all_gather x1 -> x0, waiting for transfers between devices: 46.7 us -> none  [body(): lax.all_gather(diag_inverse, 'col', axis=0, tiled=True)]
    psum x1, waiting for transfers between devices: 134 us -> 110 us  [body(): lower = lax.psum(jnp.stack(lower), AXES)]
    dynamic_update_slice x0 -> x4, local copies, waits for them, and re-layouts: none -> 5.41 us  [the longest x2 2.71 us: gather_around(): lax.dynamic_update_slice_in_dim(full, going_up, (here - far) % ways * lap...]
    ppermute x0 -> x3, starting transfers between devices: none -> 3.41 us  [the longest x1 1.83 us: gather_around(): lax.ppermute(going_down, axis, [(d, (d - 1) % ways) for d in range(ways)])]
    unnamed x8 -> x10, local copies, waits for them, and re-layouts: 7.29 us -> 7.29 us
  transfers between devices with their start and end apart: 4 -> 6, of which waited for: 3 -> 4; matrix products, arithmetic and copies ran while one was open for 5% -> 5% of each run, Pallas kernels for 0% -> 0%
where the time goes in v1:
time: 329 us; the launch traced here: 328 us
  waiting for transfers between devices  241 us (73%)
  matrix products  24.5 us (7%)
  between operations  23.5 us (7%)
  local copies, waits for them, and re-layouts  15.9 us (5%)
  starting transfers between devices  15.4 us (5%)
  other arithmetic  7.99 us (2%)
    psum x1, waiting for transfers between devices, body(): lower = lax.psum(jnp.stack(lower), AXES)  110 us
    all_gather x1, waiting for transfers between devices, body(): lax.all_gather(jnp.concatenate(solved, axis=1), AXES, axis=0, tiled=True)  79.3 us
    ppermute x2, waiting for transfers between devices, gather_around(): lax.ppermute(going_up, axis, [(d, (d + 1) % ways) for d in range(ways)])  51.5 us
    dot_general x8, matrix products, dot_nt(): return lax.dot_general(a, b, NT, preferred_element_type=jnp.float32)  24.5 us
    all_to_all x1, starting transfers between devices, body(): lax.all_to_all(right_side.T.reshape(ndev, width, panel), AXES, split_axis...  12 us
    unnamed x10, local copies, waits for them, and re-layouts  7.29 us
  transfers between devices with their start and end apart: 6, of which 4 were waited for; matrix products, arithmetic and copies ran while one was open for 5% of the time, Pallas kernels for 0%

profile of v1, /device:TPU:1, one launch (start us, length us, event | category | flops | bytes accessed | tf_op | source)
XLA Modules:
  0.0 328.4 jit_solution(10689542621531023958)
XLA Ops:
  7.2 6.4 %copy.8 = bf16[512,4096]{0,1:T(8,128)(2,1)} copy(bf16[512,4096]{1,0:T(8,128)(2,1)} %param.5) | data formatting | bytes 8388608 | tf_op args[0]
  13.6 0.0 copy-start.2
  13.6 0.0 copy-start.1
  13.6 12.0 %all-to-all-start = ((bf16[128,32,512]{2,1,0:T(8,128)(2,1)}), bf16[128,32,512]{2,1,0:T(8,128)(2,1)}, u32[]{:S(2)}, u32[]{:S(2)}) async-start(bf16[128,32,512]{2,1,0:T(8,128)(2,1)} %bitcast.72), calls=%async_computation | async-start | bytes 8388608 | tf_op jit(solution)/shard_map/all_to_all | solution.py:43
  25.5 0.0 all-reduce.2.cloned.1.call-start
  25.6 0.0 copy-done.2
  25.6 0.1 broadcast_bitcast_fusion
  25.7 0.0 copy-done.1
  25.7 0.6 fusion.16
  28.2 1.7 broadcast_select_fusion
  30.0 0.9 bitcast_dynamic-update-slice_fusion.4
  30.9 1.0 bitcast_dynamic-update-slice_fusion.3
  31.8 0.9 bitcast_dynamic-update-slice_fusion.2
  32.8 0.0 copy-start
  32.8 0.9 bitcast_dynamic-update-slice_fusion.1
  33.7 0.9 bitcast_dynamic-update-slice_fusion
  34.6 0.9 fusion.7
  35.5 0.0 all-reduce.2.cloned.1.call-update
  35.6 0.0 all-gather.2.cloned.1.call-start
  35.6 0.0 copy-done
  35.6 1.6 collective-permute-start
  37.2 1.8 collective-permute-start.1
  39.0 49.1 %collective-permute-done = bf16[512,512]{1,0:T(8,128)(2,1)S(1)} collective-permute-done((bf16[512,512]{1,0:T(8,128)(2,1)S(1)}, bf16[512,512]{1,0:T(8,128)(2,1)S(1)}, u32[]{:S(2)}, u32[]{:S(2)}) %collective-permute-start) | collective-permute-done | bytes 524320 | tf_op jit(solution)/shard_map/ppermute | solution.py:16
  88.1 0.0 collective-permute-start.2
  95.5 1.5 broadcast_in_dim.19
  97.0 0.8 constant_dynamic-update-slice_fusion.3
  97.8 0.8 constant_dynamic-update-slice_fusion.2
  98.7 0.0 collective-permute-done.1
  98.7 1.9 constant_dynamic-update-slice_fusion.1
  100.6 2.4 collective-permute-done.2
  102.9 1.9 constant_dynamic-update-slice_fusion
  104.8 0.0 all-to-all-done
  104.8 1.3 convolution_convert_fusion.3
  106.1 110.2 %all-reduce.2.cloned.1.call-done = bf16[6,512,512]{2,1,0:T(8,128)(2,1)} async-done(((bf16[6,512,512]{2,1,0:T(8,128)(2,1)}), bf16[6,512,512]{2,1,0:T(8,128)(2,1)}) %all-reduce.2.cloned.1.call-update) | async-done | bytes 3145744 | tf_op jit(solution)/shard_map/psum | solution.py:52
  216.4 1.3 convolution_subtract_fusion.4
  217.7 1.6 convolution_convert_fusion.2
  219.3 1.3 convolution_subtract_fusion.2
  220.7 1.6 convolution_convert_fusion.1
  222.3 1.3 convolution_subtract_fusion.1
  223.6 1.6 convolution_convert_fusion
  225.3 0.7 pad_maximum_fusion
  226.0 0.0 all-gather.2.cloned.1.call-update
  226.0 79.3 %all-gather.2.cloned.1.call-done = bf16[4096,2048]{1,0:T(8,128)(2,1)} async-done(((bf16[32,2048]{1,0:T(8,128)(2,1)}), bf16[4096,2048]{1,0:T(8,128)(2,1)}) %all-gather.2.cloned.1.call-update) | async-done | bytes 16777232 | tf_op jit(solution)/shard_map/all_gather | solution.py:62
  305.2 1.1 dynamic-slice_bitcast_fusion
  306.4 0.8 copy.9
  307.1 14.4 %subtract_convert_fusion = bf16[512,4096]{1,0:T(8,128)(2,1)} fusion(bf16[512,4096]{1,0:T(8,128)(2,1)} %param.5, bf16[512,2048]{1,0:T(8,128)(2,1)S(1)} %broadcast_select_fusion, bf16[4096,2048]{1,0:T(8,128)(2,1)} %all-gather.2.cloned.1.call-done), kind=kOutput, calls=%fused_computation | convolution fusion | flops 8596226048 | bytes 27262976 | tf_op jit(solution)/shard_map/dot_general | solution.py:27
  (2 shorter events, 0.0 us)
Async XLA Ops:
  13.6 12.0 %copy-start.2 = (s32[1,4]{1,0:T(1,128)S(1)}, s32[1,4]{1,0:T(1,128)}, u32[]{:S(2)}) copy-start(s32[1,4]{1,0:T(1,128)} %param.8) | copy-start | bytes 52
  13.6 12.1 %copy-start.1 = (s32[4]{0:T(128)S(1)}, s32[4]{0:T(128)}, u32[]{:S(2)}) copy-start(s32[4]{0:T(128)} %param.9) | copy-start | bytes 52
  13.6 91.2 %all-to-all-start = ((bf16[128,32,512]{2,1,0:T(8,128)(2,1)}), bf16[128,32,512]{2,1,0:T(8,128)(2,1)}, u32[]{:S(2)}, u32[]{:S(2)}) async-start(bf16[128,32,512]{2,1,0:T(8,128)(2,1)} %bitcast.72), calls=%async_computation | async-start | bytes 8388608 | tf_op jit(solution)/shard_map/all_to_all | solution.py:43
  25.5 190.8 %all-reduce.2.cloned.1.call-start = ((), (), s32[]{:S(2)}) async-start(), calls=%async_computation.1 | async-start | bytes 6291456 | tf_op jit(solution)/shard_map/psum | solution.py:52
  32.8 2.8 copy-start
  35.6 269.7 %all-gather.2.cloned.1.call-start = ((), (), s32[]{:S(2)}) async-start(), calls=%async_computation.2 | async-start | bytes 16908288 | tf_op jit(solution)/shard_map/all_gather | solution.py:62
  35.6 52.5 %collective-permute-start = (bf16[512,512]{1,0:T(8,128)(2,1)S(1)}, bf16[512,512]{1,0:T(8,128)(2,1)S(1)}, u32[]{:S(2)}, u32[]{:S(2)}) collective-permute-start(bf16[512,512]{1,0:T(8,128)(2,1)S(1)} %copy-done), channel_id=1, source_target_pairs={{0,1},{1,2},{2,3},{3,0},{4,5},{5,6},{6,7},{7,4},{8,9},{9,10},{10,1... | collective-permute-start | bytes 1572872 | tf_op jit(solution)/shard_map/ppermute | solution.py:16
  37.2 61.5 %collective-permute-start.1 = (bf16[512,512]{1,0:T(8,128)(2,1)S(1)}, bf16[512,512]{1,0:T(8,128)(2,1)}, u32[]{:S(2)}, u32[]{:S(2)}) collective-permute-start(bf16[512,512]{1,0:T(8,128)(2,1)S(1)} %copy-done), channel_id=1, source_target_pairs={{0,3},{1,0},{2,1},{3,2},{4,7},{5,4},{6,5},{7,6},{8,11},{9,8},{10,9... | collective-permute-start | bytes 1572872 | tf_op jit(solution)/shard_map/ppermute | solution.py:19
  88.1 14.8 %collective-permute-start.2 = (bf16[512,512]{1,0:T(8,128)(2,1)S(1)}, bf16[512,512]{1,0:T(8,128)(2,1)}, u32[]{:S(2)}, u32[]{:S(2)}) collective-permute-start(bf16[512,512]{1,0:T(8,128)(2,1)S(1)} %collective-permute-done), channel_id=1, source_target_pairs={{0,1},{1,2},{2,3},{3,0},{4,5},{5,6},{6,7},{7,4},{8,9},{9,10},{10,1... | collective-permute-start | bytes 1572872 | tf_op jit(solution)/shard_map/ppermute | solution.py:16
Sparse Core Ops, SparseCore 0:
  35.7 180.6 all-reduce.1
  226.1 79.0 all-gather.1

commit v2 on v0

--- a/solution.py
+++ b/solution.py
@@ -33,7 +33,7 @@
         for j in range(k):
             tile = masked[:, j * panel : (j + 1) * panel]
             lower.append(jnp.where(mine, tile, jnp.zeros_like(tile)))
-    lower = lax.psum(jnp.stack(lower), AXES)
+    lower = lax.psum(lax.psum(jnp.stack(lower), "row"), "col")
     inverses = lax.all_gather(diag_inverse, "col", axis=0, tiled=True).reshape(window, panel, panel)
     solved = []
     for k in range(window):

time: 339 us -> 359 us (1.059)
  waiting for transfers between devices: 260 us -> 278 us
    psum x1 -> x2, waiting for transfers between devices: 134 us -> 197 us  [body(): lower = lax.psum(lax.psum(jnp.stack(lower), 'row'), 'col')]
    all_gather x1, waiting for transfers between devices: 46.7 us -> 0.03 us  [body(): lax.all_gather(diag_inverse, 'col', axis=0, tiled=True)]
    unnamed x8 -> x4, local copies, waits for them, and re-layouts: 7.29 us -> 7.28 us
  transfers between devices with their start and end apart: 4 -> 5, of which waited for: 3 -> 3; matrix products, arithmetic and copies ran while one was open for 5% -> 2% of each run, Pallas kernels for 0% -> 0%
where the time goes in v2:
time: 359 us; the launch traced here: 358 us
  waiting for transfers between devices  278 us (77%)
  between operations  24.8 us (7%)
  matrix products  24.7 us (7%)
  starting transfers between devices  12.1 us (3%)
  local copies, waits for them, and re-layouts  9.79 us (3%)
  other arithmetic  8.63 us (2%)
    psum x2, waiting for transfers between devices, body(): lower = lax.psum(lax.psum(jnp.stack(lower), 'row'), 'col')  197 us
    all_gather x1, waiting for transfers between devices, body(): lax.all_gather(jnp.concatenate(solved, axis=1), AXES, axis=0, tiled=True)  80.7 us
    dot_general x8, matrix products, dot_nt(): return lax.dot_general(a, b, NT, preferred_element_type=jnp.float32)  24.7 us
    all_to_all x1, starting transfers between devices, body(): lax.all_to_all(right_side.T.reshape(ndev, width, panel), AXES, split_axis...  12 us
    unnamed x4, local copies, waits for them, and re-layouts  7.28 us
  transfers between devices with their start and end apart: 5, of which 3 were waited for; matrix products, arithmetic and copies ran while one was open for 2% of the time, Pallas kernels for 0%

profile of v2, /device:TPU:1, one launch (start us, length us, event | category | flops | bytes accessed | tf_op | source)
XLA Modules:
  0.0 358.4 jit_solution(9042539240581737296)
XLA Ops:
  8.0 0.0 all-reduce.3.cloned.1.call-start
  8.0 1.4 fusion.16
  9.5 0.7 compare_bitcast_fusion
  10.1 0.1 broadcast_bitcast_fusion
  11.5 1.7 broadcast_select_fusion
  13.2 0.9 bitcast_dynamic-update-slice_fusion.4
  14.1 0.9 bitcast_dynamic-update-slice_fusion.3
  15.1 0.9 bitcast_dynamic-update-slice_fusion.2
  16.7 0.9 bitcast_dynamic-update-slice_fusion.1
  17.6 0.9 bitcast_dynamic-update-slice_fusion
  18.5 0.9 fusion.7
  19.4 0.0 all-reduce.3.cloned.1.call-update
  19.4 0.0 all-gather.3.cloned.1.call-start
  19.5 0.5 all-gather.3.cloned.1.call-update
  20.0 6.4 %copy.8 = bf16[512,4096]{0,1:T(8,128)(2,1)} copy(bf16[512,4096]{1,0:T(8,128)(2,1)} %param.5) | data formatting | bytes 8388608 | tf_op args[0]
  26.4 12.0 %all-to-all-start = ((bf16[128,32,512]{2,1,0:T(8,128)(2,1)}), bf16[128,32,512]{2,1,0:T(8,128)(2,1)}, u32[]{:S(2)}, u32[]{:S(2)}) async-start(bf16[128,32,512]{2,1,0:T(8,128)(2,1)} %bitcast.72), calls=%async_computation | async-start | bytes 8388608 | tf_op jit(solution)/shard_map/all_to_all | solution.py:27
  38.4 0.0 all-reduce.5.cloned.1.call-start
  38.4 130.4 %all-reduce.3.cloned.1.call-done = bf16[6,512,512]{2,1,0:T(8,128)(2,1)} async-done(((bf16[6,512,512]{2,1,0:T(8,128)(2,1)}), bf16[6,512,512]{2,1,0:T(8,128)(2,1)}) %all-reduce.3.cloned.1.call-update) | async-done | bytes 3145744 | tf_op jit(solution)/shard_map/psum | solution.py:36
  168.8 0.0 all-reduce.5.cloned.1.call-update
  168.8 0.0 all-gather.5.cloned.1.call-start
  176.2 0.0 all-gather.3.cloned.1.call-done
  176.2 0.0 all-to-all-done
  176.2 1.5 convolution_convert_fusion.3
  177.7 66.7 %all-reduce.5.cloned.1.call-done = bf16[6,512,512]{2,1,0:T(8,128)(2,1)} async-done(((bf16[6,512,512]{2,1,0:T(8,128)(2,1)}), bf16[6,512,512]{2,1,0:T(8,128)(2,1)}) %all-reduce.5.cloned.1.call-update) | async-done | bytes 3145744 | tf_op jit(solution)/shard_map/psum | solution.py:36
  244.4 1.3 convolution_subtract_fusion.4
  245.7 1.6 convolution_convert_fusion.2
  247.4 1.3 convolution_subtract_fusion.2
  248.7 1.6 convolution_convert_fusion.1
  250.4 1.3 convolution_subtract_fusion.1
  251.7 1.6 convolution_convert_fusion
  253.3 0.7 pad_maximum_fusion
  254.0 0.0 all-gather.5.cloned.1.call-update
  254.1 80.7 %all-gather.5.cloned.1.call-done = bf16[4096,2048]{1,0:T(8,128)(2,1)} async-done(((bf16[32,2048]{1,0:T(8,128)(2,1)}), bf16[4096,2048]{1,0:T(8,128)(2,1)}) %all-gather.5.cloned.1.call-update) | async-done | bytes 16777232 | tf_op jit(solution)/shard_map/all_gather | solution.py:46
  334.7 1.1 dynamic-slice_bitcast_fusion
  335.8 0.8 copy.9
  336.6 14.4 %subtract_convert_fusion = bf16[512,4096]{1,0:T(8,128)(2,1)} fusion(bf16[512,4096]{1,0:T(8,128)(2,1)} %param.5, bf16[512,2048]{1,0:T(8,128)(2,1)S(1)} %broadcast_select_fusion, bf16[4096,2048]{1,0:T(8,128)(2,1)} %all-gather.5.cloned.1.call-done), kind=kOutput, calls=%fused_computation | convolution fusion | flops 8596226048 | bytes 27262976 | tf_op jit(solution)/shard_map/dot_general | solution.py:11
  (1 shorter events, 0.0 us)
Async XLA Ops:
  8.0 160.8 %all-reduce.3.cloned.1.call-start = ((), (), s32[]{:S(2)}) async-start(), calls=%async_computation.2 | async-start | bytes 6291456 | tf_op jit(solution)/shard_map/psum | solution.py:36
  19.4 156.8 %all-gather.3.cloned.1.call-start = ((), (), s32[]{:S(2)}) async-start(), calls=%async_computation.1 | async-start | bytes 2621440 | tf_op jit(solution)/shard_map/all_gather | solution.py:37
  26.4 149.8 %all-to-all-start = ((bf16[128,32,512]{2,1,0:T(8,128)(2,1)}), bf16[128,32,512]{2,1,0:T(8,128)(2,1)}, u32[]{:S(2)}, u32[]{:S(2)}) async-start(bf16[128,32,512]{2,1,0:T(8,128)(2,1)} %bitcast.72), calls=%async_computation | async-start | bytes 8388608 | tf_op jit(solution)/shard_map/all_to_all | solution.py:27
  38.4 206.1 %all-reduce.5.cloned.1.call-start = ((), (), s32[]{:S(2)}) async-start(), calls=%async_computation.3 | async-start | bytes 6291456 | tf_op jit(solution)/shard_map/psum | solution.py:36
  168.8 165.9 %all-gather.5.cloned.1.call-start = ((), (), s32[]{:S(2)}) async-start(), calls=%async_computation.4 | async-start | bytes 16908288 | tf_op jit(solution)/shard_map/all_gather | solution.py:46
Sparse Core Ops, SparseCore 0:
  19.5 149.2 all-reduce.2
  254.2 80.5 all-gather.4
Sparse Core Ops, SparseCore 1:
  21.5 78.9 all-gather.2
  168.9 75.5 all-reduce.4
